TPU v7x, 32 devices: a whole 2x2x4 slice. The times are simulated.
32 devices in a mesh: row: 8 (over z, core), col: 4 (over y, x).
Axes of the slice: x: 2, y: 2, z: 4, core: 2. Of those that a mesh axis runs over, the one named last changes fastest.
Arguments:
- matrix_tiles: float32 [10, 8, 128, 20, 4, 128], P(None, 'row', None, None, 'col'), may hold values from -60715.73 to 60715.73
Outputs:
- reduced: float32 [10, 8, 128, 20, 4, 128], P(None, 'row', None, None, 'col')
All inputs are finite; a program needn't handle non-finite values.
Results may differ from a plain program's by a relative error of at most 0.0003.
Values sent between devices are 32-bit elements; how exact they have to be, the bound alone decides.
A program may use at most 128 MiB of HBM per device.

v0:
```python
import jax
import jax.numpy as jnp
from jax import lax
from jax.sharding import PartitionSpec as P

BAND = 256
PANELS = 2


def from_root(shard, axis, root):
    mine = lax.axis_index(axis) == root
    return lax.psum(jnp.where(mine, shard, jnp.zeros_like(shard)), axis)


def multiply(first_matrix, second_matrix):
    return jnp.dot(
        first_matrix,
        second_matrix,
        precision=lax.Precision.HIGHEST,
        preferred_element_type=first_matrix.dtype,
    )


def transposed_left(first_matrix, second_matrix):
    return lax.dot_general(
        first_matrix,
        second_matrix,
        (((0,), (0,)), ((), ())),
        precision=lax.Precision.HIGHEST,
        preferred_element_type=first_matrix.dtype,
    )


def transposed_right(first_matrix, second_matrix):
    return lax.dot_general(
        first_matrix,
        second_matrix,
        (((1,), (1,)), ((), ())),
        precision=lax.Precision.HIGHEST,
        preferred_element_type=first_matrix.dtype,
    )


def lower_inverse(matrix):
    factor = jnp.linalg.cholesky(matrix)
    identity = jnp.eye(matrix.shape[0], dtype=matrix.dtype)
    return lax.linalg.triangular_solve(factor, identity, left_side=True, lower=True)


def reflector_factors(gram_matrix, top_panel):
    inverse = lower_inverse(gram_matrix)
    top_basis = transposed_right(top_panel, inverse)
    sign_values = jnp.where(jnp.diagonal(top_basis) >= 0, -1.0, 1.0).astype(top_basis.dtype)
    shifted = top_basis - jnp.diag(sign_values)
    outer_inverse = lower_inverse(transposed_left(shifted, shifted))
    kernel = transposed_left(outer_inverse, outer_inverse)
    transform = -sign_values[:, None] * multiply(shifted, kernel)
    return (inverse, sign_values, transform)


def mirror_order(pieces, block_rows, tile_size):
    stacked = jnp.stack(pieces, 0)
    stacked = stacked.reshape(len(pieces), block_rows, tile_size, stacked.shape[-1])
    return stacked.transpose(1, 0, 2, 3).reshape(-1, stacked.shape[-1])


def on_device(matrix_tiles):
    tile_shape = matrix_tiles.shape
    block_rows = tile_shape[0]
    tile_size = tile_shape[2]
    block_cols = tile_shape[3]
    row_count = block_rows * tile_size
    col_count = block_cols * tile_size
    local_block = matrix_tiles.reshape(row_count, col_count)
    row_devices = lax.axis_size("row")
    col_devices = lax.axis_size("col")
    row_ratio = row_devices // col_devices
    row_index = lax.axis_index("row")
    col_index = lax.axis_index("col")
    positions = jnp.arange(row_count, dtype=jnp.int32)
    global_rows = (
        positions // tile_size * row_devices + row_index
    ) * tile_size + positions % tile_size
    band_columns = jnp.arange(BAND, dtype=jnp.int32)
    panel_tiles = BAND // tile_size
    for panel_index in range(PANELS):
        panel_start = panel_index * BAND
        below_start = panel_start + BAND
        pieces = []
        for offset in range(panel_tiles):
            column_tile = panel_start // tile_size + offset
            local_tile = column_tile // col_devices
            source = local_block[:, local_tile * tile_size : (local_tile + 1) * tile_size]
            pieces.append(from_root(source, "col", column_tile % col_devices))
        panel_rows = jnp.concatenate(pieces, 1)
        panel_rows = jnp.where((global_rows >= below_start)[:, None], panel_rows, 0.0)
        partial_gram = transposed_left(panel_rows, panel_rows)
        gram_matrix = lax.psum(partial_gram, "row")
        blocks = []
        for offset in range(panel_tiles):
            row_tile = below_start // tile_size + offset
            local_tile = row_tile // row_devices
            source = panel_rows[local_tile * tile_size : (local_tile + 1) * tile_size]
            blocks.append(from_root(source, "row", row_tile % row_devices))
        top_panel = jnp.concatenate(blocks, 0)
        inverse, sign_values, transform = reflector_factors(gram_matrix, top_panel)
        sign_places = (global_rows[:, None] - below_start == band_columns[None, :]).astype(
            local_block.dtype
        )
        vec_rows = transposed_right(panel_rows, inverse) - sign_places * sign_values[None, :]
        pieces = []
        for part_index in range(row_ratio):
            pieces.append(from_root(vec_rows, "row", col_index + col_devices * part_index))
        vec_cols = mirror_order(pieces, block_rows, tile_size)
        summed_rows = lax.psum(multiply(local_block, vec_cols), "col")
        applied = multiply(summed_rows, transform)
        inner_term = multiply(transform.T, lax.psum(transposed_left(vec_rows, applied), "row"))
        update_rows = applied - 0.5 * multiply(vec_rows, inner_term)
        column_part = transposed_left(local_block, vec_rows)
        summed_cols = lax.psum(column_part, "row")
        update_cols = multiply(summed_cols, transform) - 0.5 * multiply(vec_cols, inner_term)
        left_factor = jnp.concatenate([vec_rows, update_rows], 1)
        right_factor = jnp.concatenate([update_cols, vec_cols], 1)
        local_block = local_block - transposed_right(left_factor, right_factor)
    return local_block.reshape(tile_shape)


def solution(mesh):
    return jax.shard_map(
        on_device,
        mesh=mesh,
        in_specs=(P(None, "row", None, None, "col", None),),
        out_specs=P(None, "row", None, None, "col", None),
        check_vma=False,
    )
```

profile of v0, /device:TPU:0, one launch (start us, length us, event | category | flops | bytes accessed | tf_op | source)
XLA Modules:
  0.0 1142.7 jit_solution(3032368912725932266)
XLA Ops:
  6.5 102.2 %reduce.8 = f32[10,128,20,128]{3,2,1,0:T(8,128)} reduce(f32[10,1,128,20,1,128]{5,4,3,2,1,0:T(1,128)} %param.4, f32[]{:T(128)} %constant.208), dimensions={1,4}, to_apply=%param.4.reduce_sub_computation | reduce | bytes 26214404 | tf_op args[0]
  108.8 13.6 %copy.28 = f32[160,8,20,128]{3,1,2,0:T(8,128)} copy(f32[160,8,20,128]{3,2,1,0:T(8,128)} %bitcast.198) | data formatting | bytes 26214400
  122.4 2.2 slice_select_fusion.3
  124.7 59.2 %all-reduce.38.cloned.1.call-done = (f32[1280,128]{1,0:T(8,128)}, f32[1280,128]{1,0:T(8,128)}) async-done(((f32[1280,128]{1,0:T(8,128)}, f32[1280,128]{1,0:T(8,128)}), (f32[1280,128]{1,0:T(8,128)}, f32[1280,128]{1,0:T(8,128)})) %all-reduce.38.cloned.1.call-update) | async-done | bytes 1310736 | tf_op jit(solution)/shard_map/psum | solution.py:12
  183.9 1.5 maximum_select_fusion
  185.4 3.0 fusion.104
  189.5 56.5 %all-reduce.34.cloned.1.call-done = (f32[128,256]{1,0:T(8,128)}, f32[128,256]{1,0:T(8,128)}, f32[256,256]{0,1:T(8,128)}) async-done(((f32[128,256]{1,0:T(8,128)}, f32[128,256]{1,0:T(8,128)}, f32[256,256]{0,1:T(8,128)}), (f32[128,256]{1,0:T(8,128)}, f32[128,256]{1,0:T(8,128)}, f32[256,256]{0,1:T(8,128)})) %all-reduce.34.cloned.1.call-update) | async-done | bytes 524304 | tf_op jit(solution)/shard_map/psum | solution.py:12
  248.1 11.7 %cholesky.214 = f32[128,128]{1,0:T(8,128)S(1)} custom-call(f32[128,128]{1,0:T(8,128)S(1)} %cholesky.346), custom_call_target="Cholesky" | custom-call | tf_op jit(solution)/shard_map/jit(cholesky)/cholesky | solution.py:45
  259.9 9.8 custom-call.21
  270.2 11.7 %cholesky.231 = f32[128,128]{1,0:T(8,128)S(1)} custom-call(f32[128,128]{1,0:T(8,128)S(1)} %convolution_subtract_fusion.11), custom_call_target="Cholesky" | custom-call | tf_op jit(solution)/shard_map/jit(cholesky)/cholesky | solution.py:45
  284.0 4.1 while.8
  288.1 19.7 %custom-call.22 = f32[2,128,128]{1,2,0:T(8,128)S(1)} custom-call(f32[2,128,128]{2,1,0:T(8,128)S(1)} %get-tuple-element.33), custom_call_target="InvertDiagBlocksLowerTriangular" | custom-call | tf_op jit(solution)/shard_map/triangular_solve/custom-call.0 | solution.py:47
  309.1 11.1 gather_fusion
  321.1 11.7 %cholesky.248 = f32[128,128]{1,0:T(8,128)S(1)} custom-call(f32[128,128]{1,0:T(8,128)S(1)} %cholesky.349), custom_call_target="Cholesky" | custom-call | tf_op jit(solution)/shard_map/jit(cholesky)/cholesky | solution.py:45
  332.9 9.8 custom-call.23
  343.2 11.7 %cholesky.265 = f32[128,128]{1,0:T(8,128)S(1)} custom-call(f32[128,128]{1,0:T(8,128)S(1)} %convolution_subtract_fusion.10), custom_call_target="Cholesky" | custom-call | tf_op jit(solution)/shard_map/jit(cholesky)/cholesky | solution.py:45
  357.6 3.6 broadcast_select_fusion.3
  361.3 4.1 while.9
  365.4 19.7 %custom-call.24 = f32[2,128,128]{1,2,0:T(8,128)S(1)} custom-call(f32[2,128,128]{2,1,0:T(8,128)S(1)} %get-tuple-element.34), custom_call_target="InvertDiagBlocksLowerTriangular" | custom-call | tf_op jit(solution)/shard_map/triangular_solve/custom-call.0 | solution.py:47
  385.7 44.1 %all-reduce.32.cloned.1.call-done = (f32[1,10,128,256]{3,2,0,1:T(8,128)}, f32[1,10,128,256]{3,2,0,1:T(8,128)}) async-done(((f32[1,10,128,256]{3,2,0,1:T(8,128)}, f32[1,10,128,256]{3,2,0,1:T(8,128)}), (f32[1,10,128,256]{3,2,0,1:T(8,128)}, f32[1,10,128,256]{3,2,0,1:T(8,128)})) %all-reduce.32.cloned.1.call-update) | async-done | bytes 2621456 | tf_op jit(solution)/shard_map/psum | solution.py:12
  429.8 2.0 pad_maximum_fusion
  431.7 25.7 %convolution_bitcast_fusion.1 = f32[1280,256]{0,1:T(8,128)} fusion(f32[2560,256]{1,0:T(8,128)S(1)} %bitcast.202, f32[1280,2560]{1,0:T(8,128)} %bitcast.193), kind=kOutput, calls=%fused_computation.30 | convolution fusion | flops 10066329600 | bytes 17039360 | tf_op jit(solution)/shard_map/dot_general | solution.py:16
  458.9 15.8 %convolution_bitcast_fusion = f32[2560,256]{0,1:T(8,128)} fusion(f32[1280,256]{1,0:T(8,128)S(1)} %copy-done.4, f32[1280,2560]{1,0:T(8,128)} %bitcast.194), kind=kOutput, calls=%fused_computation.23 | convolution fusion | flops 10066329600 | bytes 17039360 | tf_op jit(solution)/shard_map/dot_general | solution.py:25
  474.8 38.4 %all-reduce.20.cloned.1.call-done = f32[1280,256]{0,1:T(8,128)} async-done(((f32[1280,256]{0,1:T(8,128)}), f32[1280,256]{0,1:T(8,128)}) %all-reduce.20.cloned.1.call-update) | async-done | bytes 1310736 | tf_op jit(solution)/shard_map/psum | solution.py:115
  513.2 2.8 fusion.105
  517.1 3.0 fusion.106
  520.4 2.8 copy.16
  523.2 69.6 %all-reduce.30.cloned.1.call-done = (f32[2560,256]{0,1:T(8,128)}, f32[256,256]{1,0:T(8,128)}) async-done(((f32[2560,256]{0,1:T(8,128)}, f32[256,256]{1,0:T(8,128)}), (f32[2560,256]{0,1:T(8,128)}, f32[256,256]{1,0:T(8,128)})) %all-reduce.30.cloned.1.call-update) | async-done | bytes 2883600 | tf_op jit(solution)/shard_map/psum | solution.py:120
  592.8 1.5 fusion.107
  594.4 6.1 fusion.108
  601.7 2.2 fusion.7
  604.0 24.8 %convolution_subtract_fusion.1 = f32[1280,2560]{1,0:T(8,128)S(1)} fusion(f32[1280,2560]{1,0:T(8,128)} %bitcast.195, f32[2560,256]{1,0:T(8,128)S(1)} %bitcast.204, f32[2560,256]{1,0:T(8,128)S(1)} %fusion.7, f32[1280,256]{1,0:T(8,128)S(1)} %fusion.9, f32[1280,256]{1,0:T(8,128)S(1)} %copy-done.6), kind=kOutput, calls=%fused_computation.11 | convolution fusion | flops 20137902080 | bytes 34078720 | tf_op jit(solution)/shard_map/dot_general | solution.py:35
  628.8 4.9 copy-done
  635.0 56.0 %all-reduce.36.cloned.1.call-done = (f32[1280,128]{1,0:T(8,128)}, f32[1280,128]{1,0:T(8,128)}) async-done(((f32[1280,128]{1,0:T(8,128)}, f32[1280,128]{1,0:T(8,128)}), (f32[1280,128]{1,0:T(8,128)}, f32[1280,128]{1,0:T(8,128)})) %all-reduce.36.cloned.1.call-update) | async-done | bytes 1310736 | tf_op jit(solution)/shard_map/psum | solution.py:12
  690.9 1.5 maximum_select_fusion.1
  692.5 3.0 fusion.109
  696.5 56.6 %all-reduce.28.cloned.1.call-done = (f32[128,256]{1,0:T(8,128)}, f32[128,256]{1,0:T(8,128)}, f32[256,256]{0,1:T(8,128)}) async-done(((f32[128,256]{1,0:T(8,128)}, f32[128,256]{1,0:T(8,128)}, f32[256,256]{0,1:T(8,128)}), (f32[128,256]{1,0:T(8,128)}, f32[128,256]{1,0:T(8,128)}, f32[256,256]{0,1:T(8,128)})) %all-reduce.28.cloned.1.call-update) | async-done | bytes 524304 | tf_op jit(solution)/shard_map/psum | solution.py:12
  755.2 11.7 %cholesky.282 = f32[128,128]{1,0:T(8,128)S(1)} custom-call(f32[128,128]{1,0:T(8,128)S(1)} %cholesky.352), custom_call_target="Cholesky" | custom-call | tf_op jit(solution)/shard_map/jit(cholesky)/cholesky | solution.py:45
  767.0 9.8 custom-call.25
  777.3 11.7 %cholesky.299 = f32[128,128]{1,0:T(8,128)S(1)} custom-call(f32[128,128]{1,0:T(8,128)S(1)} %convolution_subtract_fusion.9), custom_call_target="Cholesky" | custom-call | tf_op jit(solution)/shard_map/jit(cholesky)/cholesky | solution.py:45
  791.7 4.1 while.10
  795.8 19.7 %custom-call.26 = f32[2,128,128]{1,2,0:T(8,128)S(1)} custom-call(f32[2,128,128]{2,1,0:T(8,128)S(1)} %get-tuple-element.35), custom_call_target="InvertDiagBlocksLowerTriangular" | custom-call | tf_op jit(solution)/shard_map/triangular_solve/custom-call.0 | solution.py:47
  816.8 2.6 gather_fusion.1
  820.2 11.7 %cholesky.316 = f32[128,128]{1,0:T(8,128)S(1)} custom-call(f32[128,128]{1,0:T(8,128)S(1)} %cholesky.355), custom_call_target="Cholesky" | custom-call | tf_op jit(solution)/shard_map/jit(cholesky)/cholesky | solution.py:45
  832.0 9.8 custom-call.27
  842.3 11.7 %cholesky.333 = f32[128,128]{1,0:T(8,128)S(1)} custom-call(f32[128,128]{1,0:T(8,128)S(1)} %convolution_subtract_fusion.8), custom_call_target="Cholesky" | custom-call | tf_op jit(solution)/shard_map/jit(cholesky)/cholesky | solution.py:45
  855.4 3.6 broadcast_select_fusion.1
  860.4 4.2 while.11
  861.1 1.4 bitcast_dynamic-update-slice_fusion.11
  864.6 19.7 %custom-call.28 = f32[2,128,128]{1,2,0:T(8,128)S(1)} custom-call(f32[2,128,128]{2,1,0:T(8,128)S(1)} %get-tuple-element.36), custom_call_target="InvertDiagBlocksLowerTriangular" | custom-call | tf_op jit(solution)/shard_map/triangular_solve/custom-call.0 | solution.py:47
  884.9 44.1 %all-reduce.26.cloned.1.call-done = (f32[1,10,128,256]{3,2,0,1:T(8,128)}, f32[1,10,128,256]{3,2,0,1:T(8,128)}) async-done(((f32[1,10,128,256]{3,2,0,1:T(8,128)}, f32[1,10,128,256]{3,2,0,1:T(8,128)}), (f32[1,10,128,256]{3,2,0,1:T(8,128)}, f32[1,10,128,256]{3,2,0,1:T(8,128)})) %all-reduce.26.cloned.1.call-update) | async-done | bytes 2621456 | tf_op jit(solution)/shard_map/psum | solution.py:12
  929.0 2.0 pad_maximum_fusion.1
  930.9 14.3 %fusion.110 = f32[1280,256]{1,0:T(8,128)} fusion(f32[1280,2560]{1,0:T(8,128)} %copy-done, f32[2560,256]{1,0:T(8,128)S(1)} %bitcast.199), kind=kOutput, calls=%fused_computation.223 | convolution fusion | flops 10066329600 | bytes 17039360 | tf_op jit(solution)/shard_map/dot_general | solution.py:16
  946.6 25.0 %fusion.114 = f32[2560,256]{1,0:T(8,128)} fusion(f32[1280,2560]{1,0:T(8,128)} %copy-done, f32[1280,256]{1,0:T(8,128)S(1)} %copy-done.1), kind=kOutput, calls=%fused_computation.227 | convolution fusion | flops 10066329600 | bytes 17039360 | tf_op jit(solution)/shard_map/dot_general | solution.py:25
  971.7 29.2 %all-reduce.22.cloned.1.call-done = f32[1280,256]{1,0:T(8,128)} async-done(((f32[1280,256]{1,0:T(8,128)}), f32[1280,256]{1,0:T(8,128)}) %all-reduce.22.cloned.1.call-update) | async-done | bytes 1310736 | tf_op jit(solution)/shard_map/psum | solution.py:115
  1000.9 2.8 fusion.111
  1004.8 3.0 fusion.112
  1007.8 2.8 copy.22
  1010.6 69.9 %all-reduce.24.cloned.1.call-done = (f32[2560,256]{1,0:T(8,128)}, f32[256,256]{1,0:T(8,128)}) async-done(((f32[2560,256]{1,0:T(8,128)}, f32[256,256]{1,0:T(8,128)}), (f32[2560,256]{1,0:T(8,128)}, f32[256,256]{1,0:T(8,128)})) %all-reduce.24.cloned.1.call-update) | async-done | bytes 2883600 | tf_op jit(solution)/shard_map/psum | solution.py:120
  1080.5 1.5 fusion.113
  1082.1 4.2 fusion.115
  1087.5 2.3 fusion.6
  1089.8 25.8 %convolution_subtract_fusion = f32[1280,2560]{1,0:T(8,128)} fusion(f32[1280,2560]{1,0:T(8,128)} %copy-done, f32[2560,256]{1,0:T(8,128)S(1)} %bitcast.201, f32[2560,256]{1,0:T(8,128)S(1)} %fusion.6, f32[1280,256]{1,0:T(8,128)S(1)} %fusion.8, f32[1280,256]{1,0:T(8,128)S(1)} %copy-done.3), kind=kOutput, calls=%fused_computation.10 | convolution fusion | flops 20137902080 | bytes 34078720 | tf_op jit(solution)/shard_map/dot_general | solution.py:35
  1115.6 19.9 %reshape.157 = f32[10,1,128,20,1,128]{5,4,3,2,1,0:T(1,128)} reshape(f32[1280,2560]{1,0:T(8,128)} %convolution_subtract_fusion) | data formatting | bytes 26214400 | tf_op jit(solution)/shard_map/reshape | solution.py:125
  (154 shorter events, 42.7 us)
Async XLA Ops:
  6.5 177.3 %all-reduce.38.cloned.1.call-start = ((), (), s32[]{:S(2)}) async-start(), calls=%async_computation.9 | async-start | bytes 2621440 | tf_op jit(solution)/shard_map/psum | solution.py:12
  124.6 121.4 %all-reduce.34.cloned.1.call-start = ((), (), s32[]{:S(2)}) async-start(), calls=%async_computation.7 | async-start | bytes 1048576 | tf_op jit(solution)/shard_map/psum | solution.py:12
  189.1 240.6 %all-reduce.32.cloned.1.call-start = ((), (), s32[]{:S(2)}) async-start(), calls=%async_computation.6 | async-start | bytes 5242880 | tf_op jit(solution)/shard_map/psum | solution.py:12
  281.9 26.7 %copy-start.11 = (f32[128,256]{1,0:T(8,128)S(1)}, f32[128,256]{1,0:T(8,128)}, u32[]{:S(2)}) copy-start(f32[128,256]{1,0:T(8,128)} %get-tuple-element.80) | copy-start | bytes 393220
  281.9 26.7 %copy-start.12 = (f32[128,256]{1,0:T(8,128)S(1)}, f32[128,256]{1,0:T(8,128)}, u32[]{:S(2)}) copy-start(f32[128,256]{1,0:T(8,128)} %get-tuple-element.81) | copy-start | bytes 393220
  361.2 152.0 %all-reduce.20.cloned.1.call-start = ((), (), s32[]{:S(2)}) async-start(), calls=%async_computation | async-start | bytes 2621440 | tf_op jit(solution)/shard_map/psum | solution.py:115
  457.5 135.3 %all-reduce.30.cloned.1.call-start = ((), (), s32[]{:S(2)}) async-start(), calls=%async_computation.5 | async-start | bytes 5767168 | tf_op jit(solution)/shard_map/psum | solution.py:120
  457.6 1.4 copy-start.4
  513.2 3.9 copy-start.5
  516.0 1.1 copy-start.7
  520.1 170.8 %all-reduce.36.cloned.1.call-start = ((), (), s32[]{:S(2)}) async-start(), calls=%async_computation.8 | async-start | bytes 2621440 | tf_op jit(solution)/shard_map/psum | solution.py:12
  594.3 6.2 copy-start.6
  594.4 6.2 copy-start.9
  628.8 5.0 copy-start
  634.9 118.2 %all-reduce.28.cloned.1.call-start = ((), (), s32[]{:S(2)}) async-start(), calls=%async_computation.4 | async-start | bytes 1048576 | tf_op jit(solution)/shard_map/psum | solution.py:12
  696.2 232.7 %all-reduce.26.cloned.1.call-start = ((), (), s32[]{:S(2)}) async-start(), calls=%async_computation.3 | async-start | bytes 5242880 | tf_op jit(solution)/shard_map/psum | solution.py:12
  789.0 27.3 %copy-start.13 = (f32[128,256]{1,0:T(8,128)S(1)}, f32[128,256]{1,0:T(8,128)}, u32[]{:S(2)}) copy-start(f32[128,256]{1,0:T(8,128)} %get-tuple-element.73) | copy-start | bytes 393220
  789.0 27.3 %copy-start.14 = (f32[128,256]{1,0:T(8,128)S(1)}, f32[128,256]{1,0:T(8,128)}, u32[]{:S(2)}) copy-start(f32[128,256]{1,0:T(8,128)} %get-tuple-element.74) | copy-start | bytes 393220
  860.3 140.5 %all-reduce.22.cloned.1.call-start = ((), (), s32[]{:S(2)}) async-start(), calls=%async_computation.1 | async-start | bytes 2621440 | tf_op jit(solution)/shard_map/psum | solution.py:115
  945.2 135.3 %all-reduce.24.cloned.1.call-start = ((), (), s32[]{:S(2)}) async-start(), calls=%async_computation.2 | async-start | bytes 5767168 | tf_op jit(solution)/shard_map/psum | solution.py:120
  945.3 1.4 copy-start.1
  1000.9 3.9 copy-start.2
  1003.7 1.1 copy-start.8
  1082.0 4.2 copy-start.3
  1082.0 4.2 copy-start.10
Sparse Core Ops, SparseCore 0:
  124.7 59.0 all-reduce.37
  189.3 56.7 all-reduce.33
  361.3 68.3 all-reduce.31
  457.6 55.5 all-reduce.19
  520.3 72.4 all-reduce.29
  635.0 55.8 all-reduce.35
  696.3 56.7 all-reduce.27
  860.5 68.4 all-reduce.25
  945.3 55.5 all-reduce.21
  1008.0 72.4 all-reduce.23
where the time goes:
time: 1150 us; the launch traced here: 1140 us
  waiting for transfers between devices  524 us (46%)
  other arithmetic  333 us (29%)
  matrix products  186 us (16%)
  local copies, waits for them, and re-layouts  78.6 us (7%)
  between operations  19.9 us (2%)
    psum x6, waiting for transfers between devices, from_root(): return lax.psum(jnp.where(mine, shard, jnp.zeros_like(shard)), axis)  316 us
    psum x2, waiting for transfers between devices, on_device(): summed_cols = lax.psum(column_part, 'row')  139 us
    another operation x27, other arithmetic, lower_inverse(): factor = jnp.linalg.cholesky(matrix)  138 us
    unnamed x1, other arithmetic  102 us
    another operation x9, other arithmetic, lower_inverse(): lax.linalg.triangular_solve(factor, identity, left_side=True, lower=True)  78.8 us
    psum x2, waiting for transfers between devices, on_device(): summed_rows = lax.psum(multiply(local_block, vec_cols), 'col')  67.6 us
    dot_general x14, matrix products, multiply(): jnp.dot(first_matrix, second_matrix, precision=lax.Precision.HIGHEST, pre...  66.7 us
    dot_general x6, matrix products, transposed_right(): lax.dot_general(first_matrix, second_matrix, (((1,), (1,)), ((), ())), pr...  58.7 us
  transfers between devices with their start and end apart: 10, of which 10 were waited for; matrix products, arithmetic and copies ran while one was open for 9% of the time, Pallas kernels for 0%

commit v1 on v0

--- a/solution.py
+++ b/solution.py
@@ -117,7 +117,7 @@
         inner_term = multiply(transform.T, lax.psum(transposed_left(vec_rows, applied), "row"))
         update_rows = applied - 0.5 * multiply(vec_rows, inner_term)
         column_part = transposed_left(local_block, vec_rows)
-        summed_cols = lax.psum(column_part, "row")
+        summed_cols = jnp.sum(lax.all_gather(column_part, "row"), axis=0)
         update_cols = multiply(summed_cols, transform) - 0.5 * multiply(vec_cols, inner_term)
         left_factor = jnp.concatenate([vec_rows, update_rows], 1)
         right_factor = jnp.concatenate([update_cols, vec_cols], 1)

time: 1150 us -> 1440 us (1.25)
  waiting for transfers between devices: 524 us -> 767 us
  local copies, waits for them, and re-layouts: 78.6 us -> 100 us
  other arithmetic: 333 us -> 353 us
    all_gather x0 -> x2, waiting for transfers between devices: none -> 362 us  [on_device(): summed_cols = jnp.sum(lax.all_gather(column_part, 'row'), axis=0)]
    psum x2, waiting for transfers between devices: 139 us -> 60.6 us  [on_device(): lax.psum(transposed_left(vec_rows, applied), 'row')]
    psum x6, waiting for transfers between devices: 316 us -> 290 us  [from_root(): return lax.psum(jnp.where(mine, shard, jnp.zeros_like(shard)), axis)]
    unnamed x31 -> x52, local copies, waits for them, and re-layouts: 20.8 us -> 44.8 us
    reduce_sum x0 -> x2, other arithmetic: none -> 18.6 us  [on_device(): summed_cols = jnp.sum(lax.all_gather(column_part, 'row'), axis=0)]
    unnamed x1 -> x2, other arithmetic: 102 us -> 102 us
  transfers between devices with their start and end apart: 10 -> 12, of which waited for: 10 -> 12; matrix products, arithmetic and copies ran while one was open for 9% -> 13% of each run, Pallas kernels for 0% -> 0%
where the time goes in v1:
time: 1440 us; the launch traced here: 1430 us
  waiting for transfers between devices  767 us (53%)
  other arithmetic  353 us (25%)
  matrix products  189 us (13%)
  local copies, waits for them, and re-layouts  100 us (7%)
  between operations  19.7 us (1%)
    all_gather x2, waiting for transfers between devices, on_device(): summed_cols = jnp.sum(lax.all_gather(column_part, 'row'), axis=0)  362 us
    psum x6, waiting for transfers between devices, from_root(): return lax.psum(jnp.where(mine, shard, jnp.zeros_like(shard)), axis)  290 us
    another operation x27, other arithmetic, lower_inverse(): factor = jnp.linalg.cholesky(matrix)  138 us
    unnamed x2, other arithmetic  102 us
    another operation x9, other arithmetic, lower_inverse(): lax.linalg.triangular_solve(factor, identity, left_side=True, lower=True)  80.2 us
    dot_general x14, matrix products, multiply(): jnp.dot(first_matrix, second_matrix, precision=lax.Precision.HIGHEST, pre...  72.1 us
    psum x2, waiting for transfers between devices, on_device(): lax.psum(transposed_left(vec_rows, applied), 'row')  60.6 us
    dot_general x10, matrix products, transposed_left(): lax.dot_general(first_matrix, second_matrix, (((0,), (0,)), ((), ())), pr...  55.4 us
  transfers between devices with their start and end apart: 12, of which 12 were waited for; matrix products, arithmetic and copies ran while one was open for 13% of the time, Pallas kernels for 0%

profile of v1, /device:TPU:0, one launch (start us, length us, event | category | flops | bytes accessed | tf_op | source)
XLA Modules:
  0.0 1430.5 jit_solution(17366650871920736703)
XLA Ops:
  6.5 102.2 %reduce.8 = f32[10,128,20,128]{3,2,1,0:T(8,128)} reduce(f32[10,1,128,20,1,128]{5,4,3,2,1,0:T(1,128)} %param.4, f32[]{:T(128)} %constant.208), dimensions={1,4}, to_apply=%param.4.reduce_sub_computation | reduce | bytes 26214404 | tf_op args[0]
  108.8 13.6 copy.48
  124.7 59.2 %all-reduce.36.cloned.1.call-done = (f32[1280,128]{1,0:T(8,128)}, f32[1280,128]{1,0:T(8,128)}) async-done(((f32[1280,128]{1,0:T(8,128)}, f32[1280,128]{1,0:T(8,128)}), (f32[1280,128]{1,0:T(8,128)}, f32[1280,128]{1,0:T(8,128)})) %all-reduce.36.cloned.1.call-update) | async-done | bytes 1310736 | tf_op jit(solution)/shard_map/psum | solution.py:12
  185.4 3.0 fusion.104
  189.7 56.3 %all-reduce.32.cloned.1.call-done = (f32[128,256]{1,0:T(8,128)}, f32[128,256]{1,0:T(8,128)}, f32[256,256]{0,1:T(8,128)}) async-done(((f32[128,256]{1,0:T(8,128)}, f32[128,256]{1,0:T(8,128)}, f32[256,256]{0,1:T(8,128)}), (f32[128,256]{1,0:T(8,128)}, f32[128,256]{1,0:T(8,128)}, f32[256,256]{0,1:T(8,128)})) %all-reduce.32.cloned.1.call-update) | async-done | bytes 524304 | tf_op jit(solution)/shard_map/psum | solution.py:12
  248.1 11.7 cholesky.214
  259.9 9.8 custom-call.21
  270.2 11.7 cholesky.231
  284.0 4.1 while.8
  288.1 19.7 %custom-call.22 = f32[2,128,128]{1,2,0:T(8,128)S(1)} custom-call(f32[2,128,128]{2,1,0:T(8,128)S(1)} %get-tuple-element.33), custom_call_target="InvertDiagBlocksLowerTriangular" | custom-call | tf_op jit(solution)/shard_map/triangular_solve/custom-call.0 | solution.py:47
  309.1 2.3 gather_fusion
  312.3 3.3 broadcast_select_fusion.3
  316.0 11.7 cholesky.248
  327.7 9.8 custom-call.23
  338.0 11.7 cholesky.265
  352.9 31.4 %all-reduce.30.cloned.1.call-done = (f32[1,10,128,256]{3,2,0,1:T(8,128)}, f32[1,10,128,256]{3,2,0,1:T(8,128)}) async-done(((f32[1,10,128,256]{3,2,0,1:T(8,128)}, f32[1,10,128,256]{3,2,0,1:T(8,128)}), (f32[1,10,128,256]{3,2,0,1:T(8,128)}, f32[1,10,128,256]{3,2,0,1:T(8,128)})) %all-reduce.30.cloned.1.call-update) | async-done | bytes 2621456 | tf_op jit(solution)/shard_map/psum | solution.py:12
  386.3 26.8 %convolution_bitcast_fusion.1 = f32[1280,256]{0,1:T(8,128)} fusion(f32[2560,256]{1,0:T(8,128)S(1)} %bitcast.210, f32[1280,2560]{1,0:T(8,128)} %bitcast.199), kind=kOutput, calls=%fused_computation.31 | convolution fusion | flops 10066329600 | bytes 17039360 | tf_op jit(solution)/shard_map/dot_general | solution.py:16
  413.2 5.9 while.9
  419.0 19.7 %custom-call.24 = f32[2,128,128]{1,2,0:T(8,128)S(1)} custom-call(f32[2,128,128]{2,1,0:T(8,128)S(1)} %get-tuple-element.34), custom_call_target="InvertDiagBlocksLowerTriangular" | custom-call | tf_op jit(solution)/shard_map/triangular_solve/custom-call.0 | solution.py:47
  442.2 26.7 %all-reduce.18.cloned.1.call-done = f32[1280,256]{0,1:T(8,128)} async-done(((f32[1280,256]{0,1:T(8,128)}), f32[1280,256]{0,1:T(8,128)}) %all-reduce.18.cloned.1.call-update) | async-done | bytes 1310736 | tf_op jit(solution)/shard_map/psum | solution.py:115
  468.9 2.8 fusion.105
  472.7 3.0 fusion.106
  475.8 15.5 %convolution_bitcast_fusion = f32[2560,256]{0,1:T(8,128)} fusion(f32[1280,256]{1,0:T(8,128)} %get-tuple-element.125, f32[1280,2560]{1,0:T(8,128)} %bitcast.200), kind=kOutput, calls=%fused_computation.24 | convolution fusion | flops 10066329600 | bytes 17039360 | tf_op jit(solution)/shard_map/dot_general | solution.py:25
  491.4 2.3 copy.31
  495.6 35.8 %all-reduce.20.cloned.1.call-done = f32[256,256]{1,0:T(8,128)} async-done(((f32[256,256]{1,0:T(8,128)}), f32[256,256]{1,0:T(8,128)}) %all-reduce.20.cloned.1.call-update) | async-done | bytes 262160 | tf_op jit(solution)/shard_map/psum | solution.py:117
  533.6 2.4 fusion.9
  536.0 181.4 %all-gather.5.cloned.1.call-done = f32[20480,256]{0,1:T(8,128)} async-done(((f32[2560,256]{0,1:T(8,128)}), f32[20480,256]{0,1:T(8,128)}) %all-gather.5.cloned.1.call-update) | async-done | bytes 20971536 | tf_op jit(solution)/shard_map/all_gather | solution.py:120
  717.4 23.4 %copy.46 = f32[32,8,8,2560]{3,2,1,0:T(8,128)S(1)} copy(f32[32,8,8,2560]{3,1,2,0:T(8,128)} %bitcast.213) | data formatting | bytes 41943040
  740.8 8.8 bitcast_reduce_fusion
  749.6 4.5 fusion.108
  754.2 2.7 fusion.7
  757.0 21.5 %convolution_subtract_fusion.1 = f32[1280,2560]{1,0:T(8,128)S(1)} fusion(f32[1280,2560]{1,0:T(8,128)S(1)} %bitcast.203, f32[2560,256]{0,1:T(8,128)S(1)} %copy-done.9, f32[2560,256]{0,1:T(8,128)S(1)} %fusion.7, f32[1280,256]{1,0:T(8,128)S(1)} %copy-done.11, f32[1280,256]{1,0:T(8,128)S(1)} %copy-done.4), kind=kOutput, calls=%fused_computation.12 | convolution fusion | flops 20137902080 | bytes 34078720 | tf_op jit(solution)/shard_map/dot_general | solution.py:35
  778.5 4.9 copy-done
  784.7 54.6 %all-reduce.34.cloned.1.call-done = (f32[1280,128]{1,0:T(8,128)}, f32[1280,128]{1,0:T(8,128)}) async-done(((f32[1280,128]{1,0:T(8,128)}, f32[1280,128]{1,0:T(8,128)}), (f32[1280,128]{1,0:T(8,128)}, f32[1280,128]{1,0:T(8,128)})) %all-reduce.34.cloned.1.call-update) | async-done | bytes 1310736 | tf_op jit(solution)/shard_map/psum | solution.py:12
  840.8 3.0 fusion.109
  844.6 56.8 %all-reduce.28.cloned.1.call-done = (f32[128,256]{1,0:T(8,128)}, f32[128,256]{1,0:T(8,128)}, f32[256,256]{0,1:T(8,128)}) async-done(((f32[128,256]{1,0:T(8,128)}, f32[128,256]{1,0:T(8,128)}, f32[256,256]{0,1:T(8,128)}), (f32[128,256]{1,0:T(8,128)}, f32[128,256]{1,0:T(8,128)}, f32[256,256]{0,1:T(8,128)})) %all-reduce.28.cloned.1.call-update) | async-done | bytes 524304 | tf_op jit(solution)/shard_map/psum | solution.py:12
  903.5 11.7 cholesky.282
  915.3 9.8 custom-call.25
  925.6 11.7 cholesky.299
  940.0 4.3 while.10
  944.3 19.7 %custom-call.26 = f32[2,128,128]{1,2,0:T(8,128)S(1)} custom-call(f32[2,128,128]{2,1,0:T(8,128)S(1)} %get-tuple-element.35), custom_call_target="InvertDiagBlocksLowerTriangular" | custom-call | tf_op jit(solution)/shard_map/triangular_solve/custom-call.0 | solution.py:47
  965.4 2.3 gather_fusion.1
  968.4 3.2 broadcast_select_fusion.1
  971.9 11.7 cholesky.316
  983.7 9.8 custom-call.27
  994.0 11.7 cholesky.333
  1009.1 31.3 %all-reduce.26.cloned.1.call-done = (f32[1,10,128,256]{3,2,0,1:T(8,128)}, f32[1,10,128,256]{3,2,0,1:T(8,128)}) async-done(((f32[1,10,128,256]{3,2,0,1:T(8,128)}, f32[1,10,128,256]{3,2,0,1:T(8,128)}), (f32[1,10,128,256]{3,2,0,1:T(8,128)}, f32[1,10,128,256]{3,2,0,1:T(8,128)})) %all-reduce.26.cloned.1.call-update) | async-done | bytes 2621456 | tf_op jit(solution)/shard_map/psum | solution.py:12
  1042.3 14.4 %fusion.110 = f32[1280,256]{1,0:T(8,128)} fusion(f32[1280,2560]{1,0:T(8,128)} %copy-done, f32[2560,256]{1,0:T(8,128)S(1)} %bitcast.207), kind=kOutput, calls=%fused_computation.224 | convolution fusion | flops 10066329600 | bytes 17039360 | tf_op jit(solution)/shard_map/dot_general | solution.py:16
  1056.9 5.6 while.11
  1062.4 19.7 %custom-call.28 = f32[2,128,128]{1,2,0:T(8,128)S(1)} custom-call(f32[2,128,128]{2,1,0:T(8,128)S(1)} %get-tuple-element.36), custom_call_target="InvertDiagBlocksLowerTriangular" | custom-call | tf_op jit(solution)/shard_map/triangular_solve/custom-call.0 | solution.py:47
  1084.9 27.7 %all-reduce.22.cloned.1.call-done = f32[1280,256]{1,0:T(8,128)} async-done(((f32[1280,256]{1,0:T(8,128)}), f32[1280,256]{1,0:T(8,128)}) %all-reduce.22.cloned.1.call-update) | async-done | bytes 1310736 | tf_op jit(solution)/shard_map/psum | solution.py:115
  1112.6 2.8 fusion.111
  1116.4 3.0 fusion.112
  1119.5 25.3 %fusion.114 = f32[2560,256]{1,0:T(8,128)} fusion(f32[1280,2560]{1,0:T(8,128)} %copy-done, f32[1280,256]{1,0:T(8,128)} %get-tuple-element.130), kind=kOutput, calls=%fused_computation.228 | convolution fusion | flops 10066329600 | bytes 17039360 | tf_op jit(solution)/shard_map/dot_general | solution.py:25
  1144.8 2.5 copy.39
  1147.3 2.9 copy.38
  1150.2 24.8 %all-reduce.24.cloned.1.call-done = f32[256,256]{1,0:T(8,128)} async-done(((f32[256,256]{1,0:T(8,128)}), f32[256,256]{1,0:T(8,128)}) %all-reduce.24.cloned.1.call-update) | async-done | bytes 262160 | tf_op jit(solution)/shard_map/psum | solution.py:117
  1176.6 4.0 fusion.8
  1180.6 180.5 %all-gather.7.cloned.1.call-done = f32[20480,256]{1,0:T(8,128)} async-done(((f32[2560,256]{1,0:T(8,128)}), f32[20480,256]{1,0:T(8,128)}) %all-gather.7.cloned.1.call-update) | async-done | bytes 20971536 | tf_op jit(solution)/shard_map/all_gather | solution.py:120
  1361.1 9.7 reduce_sum.19
  1370.8 4.3 fusion.115
  1375.2 2.7 fusion.6
  1377.9 25.7 %convolution_subtract_fusion = f32[1280,2560]{1,0:T(8,128)} fusion(f32[1280,2560]{1,0:T(8,128)} %copy-done, f32[2560,256]{0,1:T(8,128)S(1)} %copy-done.10, f32[2560,256]{0,1:T(8,128)S(1)} %fusion.6, f32[1280,256]{1,0:T(8,128)S(1)} %copy-done.12, f32[1280,256]{1,0:T(8,128)S(1)} %copy-done.6), kind=kOutput, calls=%fused_computation.11 | convolution fusion | flops 20137902080 | bytes 34078720 | tf_op jit(solution)/shard_map/dot_general | solution.py:35
  1403.6 19.9 %reshape.159 = f32[10,1,128,20,1,128]{5,4,3,2,1,0:T(1,128)} reshape(f32[1280,2560]{1,0:T(8,128)} %convolution_subtract_fusion) | data formatting | bytes 26214400 | tf_op jit(solution)/shard_map/reshape | solution.py:125
  (186 shorter events, 62.9 us)
Async XLA Ops:
  6.5 177.4 %all-reduce.36.cloned.1.call-start = ((), (), s32[]{:S(2)}) async-start(), calls=%async_computation.11 | async-start | bytes 2621440 | tf_op jit(solution)/shard_map/psum | solution.py:12
  124.6 121.4 %all-reduce.32.cloned.1.call-start = ((), (), s32[]{:S(2)}) async-start(), calls=%async_computation.9 | async-start | bytes 1048576 | tf_op jit(solution)/shard_map/psum | solution.py:12
  189.2 195.2 %all-reduce.30.cloned.1.call-start = ((), (), s32[]{:S(2)}) async-start(), calls=%async_computation.8 | async-start | bytes 5242880 | tf_op jit(solution)/shard_map/psum | solution.py:12
  281.9 26.8 %copy-start.17 = (f32[128,256]{1,0:T(8,128)S(1)}, f32[128,256]{1,0:T(8,128)}, u32[]{:S(2)}) copy-start(f32[128,256]{1,0:T(8,128)} %get-tuple-element.76) | copy-start | bytes 393220
  281.9 26.8 %copy-start.18 = (f32[128,256]{1,0:T(8,128)S(1)}, f32[128,256]{1,0:T(8,128)}, u32[]{:S(2)}) copy-start(f32[128,256]{1,0:T(8,128)} %get-tuple-element.77) | copy-start | bytes 393220
  315.7 153.2 %all-reduce.18.cloned.1.call-start = ((), (), s32[]{:S(2)}) async-start(), calls=%async_computation | async-start | bytes 2621440 | tf_op jit(solution)/shard_map/psum | solution.py:115
  386.3 105.1 %copy-start.1 = (f32[2,10,128,256]{3,2,0,1:T(8,128)}, f32[2,10,128,256]{3,2,0,1:T(8,128)S(1)}, u32[]{:S(2)}) copy-start(f32[2,10,128,256]{3,2,0,1:T(8,128)S(1)} %pad_maximum_fusion) | copy-start | bytes 7864324
  413.1 118.3 %all-reduce.20.cloned.1.call-start = ((), (), s32[]{:S(2)}) async-start(), calls=%async_computation.1 | async-start | bytes 524288 | tf_op jit(solution)/shard_map/psum | solution.py:117
  468.9 3.8 copy-start.3
  471.7 1.0 copy-start.7
  475.8 241.6 %all-gather.5.cloned.1.call-start = ((), (), s32[]{:S(2)}) async-start(), calls=%async_computation.4 | async-start | bytes 23592960 | tf_op jit(solution)/shard_map/all_gather | solution.py:120
  491.4 348.0 %all-reduce.34.cloned.1.call-start = ((), (), s32[]{:S(2)}) async-start(), calls=%async_computation.10 | async-start | bytes 2621440 | tf_op jit(solution)/shard_map/psum | solution.py:12
  493.8 37.6 %copy-start.13 = (f32[256,256]{1,0:T(8,128)S(1)}, f32[256,256]{1,0:T(8,128)}, u32[]{:S(2)}) copy-start(f32[256,256]{1,0:T(8,128)} %convolution_multiply_fusion.5) | copy-start | bytes 786436
  493.8 39.9 %copy-start.4 = (f32[1280,256]{1,0:T(8,128)S(1)}, f32[1280,256]{1,0:T(8,128)}, u32[]{:S(2)}) copy-start(f32[1280,256]{1,0:T(8,128)} %get-tuple-element.125) | copy-start | bytes 3932164
  532.9 0.7 copy-start.15
  740.8 8.9 copy-start.14
  740.8 16.1 %slice-start = ((s8[13107200]{0:T(1024)(128)(4,1)}), s8[4194304]{0:T(1024)(128)(4,1)S(1)}, s32[]{:S(2)}) async-start(s8[13107200]{0:T(1024)(128)(4,1)} %bitcast.201), calls=%async_computation.12 | async-start | bytes 8388608
  740.8 16.1 %slice-start.1 = ((s8[13107200]{0:T(1024)(128)(4,1)}), s8[4194304]{0:T(1024)(128)(4,1)S(1)}, s32[]{:S(2)}) async-start(s8[13107200]{0:T(1024)(128)(4,1)} %bitcast.201), calls=%async_computation.13 | async-start | bytes 8388608
  740.8 16.1 %slice-start.2 = ((s8[13107200]{0:T(1024)(128)(4,1)}), s8[4194304]{0:T(1024)(128)(4,1)S(1)}, s32[]{:S(2)}) async-start(s8[13107200]{0:T(1024)(128)(4,1)} %bitcast.201), calls=%async_computation.14 | async-start | bytes 8388608
  749.6 4.5 copy-start.2
  749.6 4.5 copy-start.16
  749.6 7.3 slice-start.3
  754.1 2.8 copy-start.9
  754.2 2.8 copy-start.11
  778.5 5.0 copy-start
  784.6 116.8 %all-reduce.28.cloned.1.call-start = ((), (), s32[]{:S(2)}) async-start(), calls=%async_computation.7 | async-start | bytes 1048576 | tf_op jit(solution)/shard_map/psum | solution.py:12
  844.6 195.8 %all-reduce.26.cloned.1.call-start = ((), (), s32[]{:S(2)}) async-start(), calls=%async_computation.6 | async-start | bytes 5242880 | tf_op jit(solution)/shard_map/psum | solution.py:12
  937.4 27.5 %copy-start.19 = (f32[128,256]{1,0:T(8,128)S(1)}, f32[128,256]{1,0:T(8,128)}, u32[]{:S(2)}) copy-start(f32[128,256]{1,0:T(8,128)} %get-tuple-element.71) | copy-start | bytes 393220
  937.4 27.6 %copy-start.20 = (f32[128,256]{1,0:T(8,128)S(1)}, f32[128,256]{1,0:T(8,128)}, u32[]{:S(2)}) copy-start(f32[128,256]{1,0:T(8,128)} %get-tuple-element.72) | copy-start | bytes 393220
  971.8 140.8 %all-reduce.22.cloned.1.call-start = ((), (), s32[]{:S(2)}) async-start(), calls=%async_computation.2 | async-start | bytes 2621440 | tf_op jit(solution)/shard_map/psum | solution.py:115
  1056.8 118.2 %all-reduce.24.cloned.1.call-start = ((), (), s32[]{:S(2)}) async-start(), calls=%async_computation.3 | async-start | bytes 524288 | tf_op jit(solution)/shard_map/psum | solution.py:117
  1112.6 3.8 copy-start.5
  1115.4 1.0 copy-start.8
  1119.5 241.6 %all-gather.7.cloned.1.call-start = ((), (), s32[]{:S(2)}) async-start(), calls=%async_computation.5 | async-start | bytes 23592960 | tf_op jit(solution)/shard_map/all_gather | solution.py:120
  1375.1 2.8 copy-start.6
  1375.2 2.8 copy-start.10
  1375.2 2.8 copy-start.12
Sparse Core Ops, SparseCore 0:
  124.8 59.0 all-reduce.35
  189.3 56.6 all-reduce.31
  315.8 68.4 all-reduce.29
  413.2 55.6 all-reduce.17
  475.9 55.4 all-reduce.19
  532.8 184.4 all-gather.4
  784.7 54.5 all-reduce.33
  844.7 56.7 all-reduce.27
  971.9 68.4 all-reduce.25
  1056.9 55.6 all-reduce.21
  1119.6 55.3 all-reduce.23
  1176.5 184.4 all-gather.6
